TPU v7x, 256 devices: a whole 4x4x8 slice. The times are simulated.
256 devices in a mesh: gx: 16 (over x, z_hi), gy: 4 (over y), gz: 4 (over z_lo, core).
Axes of the slice: x: 4, y: 4, z: 8 (z_hi: 4, z_lo: 2; z = z_hi * 2 + z_lo), core: 2. Of those that a mesh axis runs over, the one named last changes fastest.
Arguments:
- flow_field: bfloat16 [512, 256, 2048], P('gx', 'gy', 'gz'), may hold values from -96 to 96
- left_x: bfloat16 [512, 128], P('gx'), may hold values from -0.0234375 to 0.0234375
- last_x: bfloat16 [512, 128], P('gx'), may hold values from -0.25 to 0.25
- last_y: bfloat16 [256, 128], P('gy'), may hold values from -0.005859375 to 0.005859375
- right_y: bfloat16 [256, 256], P('gy'), may hold values from -0.375 to 0.375
- right_m: bfloat16 [2048, 256], P('gz'), may hold values from -0.125 to 0.125
- last_m: bfloat16 [2048, 256], P('gz'), may hold values from -0.125 to 0.125
Outputs:
- core_first: float32 [512, 128], P('gx')
- core_middle: float32 [128, 256, 128], P(('gx', 'gz'), 'gy')
- core_last: float32 [128, 2048], P(None, 'gz')
All inputs are finite; a program needn't handle non-finite values.
Results may differ from a plain program's by a relative error of at most 0.0053.
Values sent between devices are 32-bit elements; how exact they have to be, the bound alone decides.
A program may use at most 64 MiB of HBM per device.

v0:
```python
import jax
import jax.numpy as jnp
from jax import lax
from jax.sharding import PartitionSpec as P


def normal_solve(system, right_side):
    gram_matrix = jnp.dot(system, system.T, precision=lax.Precision.HIGHEST)
    factor = jnp.linalg.cholesky(gram_matrix)
    return jax.scipy.linalg.cho_solve((factor, True), right_side)


def per_device(flow_field, left_x, last_x, last_y, right_y, right_m, last_m):
    highest = lax.Precision.HIGHEST
    x_cells, y_cells, m_cells = flow_field.shape
    rank_cols = left_x.shape[1]
    sketch_cols = right_m.shape[1]
    flat_field = flow_field.reshape(x_cells * y_cells, m_cells)
    first_terms = jnp.dot(flat_field, right_m, preferred_element_type=jnp.float32).reshape(
        x_cells, y_cells, sketch_cols
    )
    first_part = jnp.sum(first_terms * right_y.astype(jnp.float32)[None], axis=1)
    first_rows = lax.psum(first_part, ("gy", "gz"))
    left_wide = left_x.astype(jnp.float32)
    first_gram = lax.psum(jnp.dot(left_wide.T, first_rows, precision=highest), "gx")
    core_first = normal_solve(first_gram, jnp.dot(first_gram, first_rows.T, precision=highest)).T
    khatri = (last_x.astype(jnp.float32)[:, None, :] * last_y.astype(jnp.float32)[None]).astype(
        jnp.bfloat16
    )
    khatri = khatri.reshape(x_cells * y_cells, rank_cols)
    last_part = jnp.dot(khatri.T, flat_field, preferred_element_type=jnp.float32)
    core_last = lax.psum(last_part, ("gx", "gy"))
    last_gram = lax.psum(jnp.dot(core_last, last_m.astype(jnp.float32), precision=highest), "gz")
    pinv_last = normal_solve(last_gram, last_gram).T
    flat_terms = jnp.dot(flat_field, last_m, preferred_element_type=jnp.float32)
    last_terms = flat_terms.reshape(x_cells, y_cells * sketch_cols)
    row_share = rank_cols // lax.axis_size(("gx", "gz"))
    middle_sums = lax.psum_scatter(
        jnp.dot(left_wide.T, last_terms, precision=highest).reshape(
            row_share * lax.axis_size(("gx", "gz")), y_cells, sketch_cols
        ),
        ("gx", "gz"),
        scatter_dimension=0,
        tiled=True,
    )
    core_middle = jnp.dot(
        middle_sums.reshape(row_share * y_cells, sketch_cols), pinv_last, precision=highest
    )
    core_middle = core_middle.reshape(row_share, y_cells, rank_cols)
    return (core_first, core_middle, core_last)


def solution(mesh):
    return jax.shard_map(
        per_device,
        mesh=mesh,
        in_specs=(
            P("gx", "gy", "gz"),
            P("gx", None),
            P("gx", None),
            P("gy", None),
            P("gy", None),
            P("gz", None),
            P("gz", None),
        ),
        out_specs=(P("gx", None), P(("gx", "gz"), "gy", None), P(None, "gz")),
        check_vma=False,
    )
```

profile of v0, /device:TPU:1, one launch (start us, length us, event | category | flops | bytes accessed | tf_op | source)
XLA Modules:
  0.0 930.0 jit_solution(4668367135638992668)
XLA Ops:
  8.0 0.0 copy-start
  8.0 0.0 copy-start.4
  8.0 0.0 copy-start.5
  8.0 0.0 all-reduce.6.cloned.1.call-start
  8.1 0.9 convert_element_type.16
  9.0 0.7 convert_element_type.15
  9.7 0.0 copy-done
  9.7 1.2 convolution_bitcast_fusion
  10.8 0.0 all-reduce.6.cloned.1.call-update
  10.9 0.0 all-reduce.4.cloned.1.call-start
  10.9 0.0 copy-start.3
  11.0 0.0 copy-start.2
  11.0 0.7 multiply_reduce_fusion
  11.7 54.8 %psum.28 = f32[32,256]{1,0:T(8,128)S(1)} all-reduce(f32[32,256]{1,0:T(8,128)S(1)} %multiply_reduce_fusion), channel_id=1, replica_groups=mesh['gx'=16,'gy'=4,'gz'=4] {'gy','gz'}, use_global_device_ids=true, to_apply=%region_1.0 | all-reduce | flops 8192 | bytes 65536 | tf_op jit(solution)/shard_map/psum | solution.py:23
  66.5 0.9 convolution_bitcast_fusion.2
  67.5 0.0 all-reduce.4.cloned.1.call-update
  67.5 0.0 all-reduce.8.cloned.1.call-start
  67.5 2.0 fusion.16
  69.5 2.8 reshape.46
  72.3 589.0 %all-reduce.6.cloned.1.call-done = f32[128,512]{1,0:T(8,128)} async-done(((f32[128,512]{1,0:T(8,128)}), f32[128,512]{1,0:T(8,128)}) %all-reduce.6.cloned.1.call-update) | async-done | bytes 262160 | tf_op jit(solution)/shard_map/psum | solution.py:32
  661.3 1.9 fusion.18
  663.2 0.0 all-reduce.8.cloned.1.call-update
  663.3 0.0 reduce-scatter.2.cloned.1.call-start
  663.3 10.1 %fusion.17 = f32[16384,128]{1,0:T(8,128)} fusion(f32[32,16384]{1,0:T(8,128)} %reshape.46, bf16[32,128]{1,0:T(8,128)(2,1)S(1)} %copy-done.3), kind=kOutput, calls=%fused_computation.32 | convolution fusion | flops 805306368 | bytes 10493952 | tf_op jit(solution)/shard_map/dot_general | solution.py:39
  673.4 9.2 copy.11
  682.6 0.0 reduce-scatter.2.cloned.1.call-update
  682.6 161.7 %all-reduce.4.cloned.1.call-done = f32[128,256]{0,1:T(8,128)} async-done(((f32[128,256]{0,1:T(8,128)}), f32[128,256]{0,1:T(8,128)}) %all-reduce.4.cloned.1.call-update) | async-done | bytes 131088 | tf_op jit(solution)/shard_map/psum | solution.py:25
  844.3 1.4 fusion.14
  845.6 0.1 copy.10
  845.8 11.7 %cholesky.44 = f32[128,128]{1,0:T(8,128)S(1)} custom-call(f32[128,128]{1,0:T(8,128)S(1)} %fusion.13), custom_call_target="Cholesky" | custom-call | tf_op jit(solution)/shard_map/jit(cholesky)/cholesky | solution.py:9
  857.5 0.6 compare_reduce_fusion.1
  858.1 0.7 fusion.3
  858.8 9.8 %custom-call.16 = f32[1,128,128]{1,2,0:T(8,128)S(1)} custom-call(f32[1,128,128]{2,1,0:T(8,128)S(1)} %fusion.3), custom_call_target="InvertDiagBlocksLowerTriangular" | custom-call | tf_op jit(solution)/shard_map/jit(_cho_solve)/triangular_solve | solution.py:10
  868.6 1.3 fusion.15
  869.9 0.3 fusion.11
  870.2 0.9 fusion.9
  871.1 23.5 %all-reduce.8.cloned.1.call-done = f32[128,256]{1,0:T(8,128)} async-done(((f32[128,256]{1,0:T(8,128)}), f32[128,256]{1,0:T(8,128)}) %all-reduce.8.cloned.1.call-update) | async-done | bytes 131088 | tf_op jit(solution)/shard_map/psum | solution.py:33
  894.5 1.3 fusion.19
  895.8 0.1 copy.12
  895.9 11.7 %cholesky.55 = f32[128,128]{1,0:T(8,128)S(1)} custom-call(f32[128,128]{1,0:T(8,128)S(1)} %fusion.8), custom_call_target="Cholesky" | custom-call | tf_op jit(solution)/shard_map/jit(cholesky)/cholesky | solution.py:9
  907.7 0.6 compare_reduce_fusion
  908.3 0.7 fusion.4
  909.0 9.8 %custom-call.17 = f32[1,128,128]{1,2,0:T(8,128)S(1)} custom-call(f32[1,128,128]{2,1,0:T(8,128)S(1)} %fusion.4), custom_call_target="InvertDiagBlocksLowerTriangular" | custom-call | tf_op jit(solution)/shard_map/jit(_cho_solve)/triangular_solve | solution.py:10
  918.8 1.2 fusion.6
  920.0 0.3 convolution_bitcast_fusion.1
  920.3 0.0 reduce-scatter.2.cloned.1.call-done
  920.3 1.8 fusion.20
  922.1 0.7 copy.16
  (11 shorter events, 0.1 us)
Async XLA Ops:
  8.0 1.7 copy-start
  8.0 2.9 copy-start.4
  8.0 2.9 copy-start.5
  8.0 653.3 %all-reduce.6.cloned.1.call-start = ((), (), s32[]{:S(2)}) async-start(), calls=%async_computation.3 | async-start | bytes 524288 | tf_op jit(solution)/shard_map/psum | solution.py:32
  10.9 833.4 %all-reduce.4.cloned.1.call-start = ((), (), s32[]{:S(2)}) async-start(), calls=%async_computation.1 | async-start | bytes 262144 | tf_op jit(solution)/shard_map/psum | solution.py:25
  10.9 55.6 %copy-start.3 = (bf16[32,128]{1,0:T(8,128)(2,1)S(1)}, bf16[32,128]{1,0:T(8,128)(2,1)}, u32[]{:S(2)}) copy-start(bf16[32,128]{1,0:T(8,128)(2,1)} %param.9) | copy-start | bytes 24580
  11.0 56.6 %copy-start.2 = (bf16[512,256]{1,0:T(8,128)(2,1)S(1)}, bf16[512,256]{1,0:T(8,128)(2,1)}, u32[]{:S(2)}) copy-start(bf16[512,256]{1,0:T(8,128)(2,1)} %param.14) | copy-start | bytes 786436
  67.5 827.1 %all-reduce.8.cloned.1.call-start = ((), (), s32[]{:S(2)}) async-start(), calls=%async_computation.4 | async-start | bytes 262144 | tf_op jit(solution)/shard_map/psum | solution.py:33
  663.3 257.1 %reduce-scatter.2.cloned.1.call-start = ((), (), s32[]{:S(2)}) async-start(), calls=%async_computation.2 | async-start | bytes 8519680 | tf_op jit(solution)/shard_map/reduce_scatter | solution.py:38
  682.6 239.5 %copy-start.1 = (f32[128,512]{1,0:T(8,128)S(1)}, f32[128,512]{1,0:T(8,128)}, u32[]{:S(2)}) copy-start(f32[128,512]{1,0:T(8,128)} %all-reduce.6.cloned.1.call-done) | copy-start | bytes 786436
Sparse Core Ops, SparseCore 0:
  12.1 649.2 all-reduce.5
  664.1 180.0 all-reduce.3
  847.7 46.8 all-reduce.7
Sparse Core Ops, SparseCore 1:
  682.7 170.6 reduce-scatter.1
where the time goes:
time: 930 us
  waiting for transfers between devices  774 us (83%)
  blocking collectives  54.8 us (6%)
  other arithmetic  47.3 us (5%)
  matrix products  25.1 us (3%)
  between operations  15.4 us (2%)
  local copies, waits for them, and re-layouts  12.9 us (1%)
    psum x1, waiting for transfers between devices, per_device(): core_last = lax.psum(last_part, ('gx', 'gy'))  589 us
    psum x1, waiting for transfers between devices, per_device(): lax.psum(jnp.dot(left_wide.T, first_rows, precision=highest), 'gx')  162 us
    psum x1, blocking collectives, per_device(): first_rows = lax.psum(first_part, ('gy', 'gz'))  54.8 us
    another operation x6, other arithmetic, normal_solve(): factor = jnp.linalg.cholesky(gram_matrix)  24.8 us
    psum x1, waiting for transfers between devices, per_device(): lax.psum(jnp.dot(core_last, last_m.astype(jnp.float32), precision=highest...  23.5 us
    another operation x4, other arithmetic, normal_solve(): return jax.scipy.linalg.cho_solve((factor, True), right_side)  20.9 us
  transfers between devices with their start and end apart: 4, of which 3 were waited for; matrix products, arithmetic and copies ran while one was open for 9% of the time, Pallas kernels for 0%

commit v1 on v0

--- a/solution.py
+++ b/solution.py
@@ -29,7 +29,7 @@
     )
     khatri = khatri.reshape(x_cells * y_cells, rank_cols)
     last_part = jnp.dot(khatri.T, flat_field, preferred_element_type=jnp.float32)
-    core_last = lax.psum(last_part, ("gx", "gy"))
+    core_last = lax.psum(lax.psum(last_part, "gx"), "gy")
     last_gram = lax.psum(jnp.dot(core_last, last_m.astype(jnp.float32), precision=highest), "gz")
     pinv_last = normal_solve(last_gram, last_gram).T
     flat_terms = jnp.dot(flat_field, last_m, preferred_element_type=jnp.float32)

time: 930 us -> 467 us (0.50)
  waiting for transfers between devices: 774 us -> 308 us
    psum x1, waiting for transfers between devices: 589 us -> 49.9 us  [per_device(): core_last = lax.psum(lax.psum(last_part, 'gx'), 'gy')]
    reduce_scatter x1, waiting for transfers between devices: 0.03 us -> 98.3 us  [per_device(): lax.psum_scatter(jnp.dot(left_wide.T, last_terms, precision=highest).resh...]
    psum x1, waiting for transfers between devices: 23.5 us -> 0.01 us  [per_device(): lax.psum(jnp.dot(core_last, last_m.astype(jnp.float32), precision=highest...]
  transfers between devices with their start and end apart: 4 -> 4, of which waited for: 3 -> 3; matrix products, arithmetic and copies ran while one was open for 9% -> 16% of each run, Pallas kernels for 0% -> 0%
where the time goes in v1:
time: 467 us; the launch traced here: 463 us
  waiting for transfers between devices  308 us (66%)
  blocking collectives  53.8 us (12%)
  other arithmetic  46.6 us (10%)
  matrix products  24.2 us (5%)
  between operations  15.4 us (3%)
  local copies, waits for them, and re-layouts  14.4 us (3%)
    psum x1, waiting for transfers between devices, per_device(): lax.psum(jnp.dot(left_wide.T, first_rows, precision=highest), 'gx')  160 us
    reduce_scatter x1, waiting for transfers between devices, per_device(): lax.psum_scatter(jnp.dot(left_wide.T, last_terms, precision=highest).resh...  98.3 us
    psum x1, blocking collectives, per_device(): first_rows = lax.psum(first_part, ('gy', 'gz'))  53.8 us
    psum x1, waiting for transfers between devices, per_device(): core_last = lax.psum(lax.psum(last_part, 'gx'), 'gy')  49.9 us
    another operation x6, other arithmetic, normal_solve(): factor = jnp.linalg.cholesky(gram_matrix)  24.8 us
    another operation x4, other arithmetic, normal_solve(): return jax.scipy.linalg.cho_solve((factor, True), right_side)  20.9 us
    dot_general x1, matrix products, per_device(): jnp.dot(left_wide.T, last_terms, precision=highest)  10.1 us
  transfers between devices with their start and end apart: 4, of which 3 were waited for; matrix products, arithmetic and copies ran while one was open for 16% of the time, Pallas kernels for 0%

profile of v1, /device:TPU:1, one launch (start us, length us, event | category | flops | bytes accessed | tf_op | source)
XLA Modules:
  0.0 462.7 jit_solution(9126587958095260097)
XLA Ops:
  8.0 0.0 copy-start
  8.0 0.0 all-reduce.9.cloned.1.call-start
  8.1 0.9 convert_element_type.14
  9.0 0.6 copy-done
  9.6 1.7 multiply_reduce_fusion
  11.3 0.0 copy-start.3
  11.3 53.8 %psum.35 = f32[32,256]{1,0:T(8,128)S(1)} all-reduce(f32[32,256]{1,0:T(8,128)S(1)} %multiply_reduce_fusion), channel_id=1, replica_groups=mesh['gx'=16,'gy'=4,'gz'=4] {'gy','gz'}, use_global_device_ids=true, to_apply=%region_1.0 | all-reduce | flops 8192 | bytes 65536 | tf_op jit(solution)/shard_map/psum | solution.py:23
  65.2 0.0 copy-done.5
  65.2 0.0 copy-done.6
  65.2 0.0 copy-done.4
  65.2 0.9 convolution_bitcast_fusion.2
  66.1 1.2 convolution_bitcast_fusion
  67.3 0.0 all-reduce.9.cloned.1.call-update
  67.3 0.0 all-reduce.5.cloned.1.call-start
  67.4 159.9 %all-reduce.9.cloned.1.call-done = (f32[128,256]{0,1:T(8,128)}, f32[128,512]{1,0:T(8,128)}) async-done(((f32[128,256]{0,1:T(8,128)}, f32[128,512]{1,0:T(8,128)}), (f32[128,256]{0,1:T(8,128)}, f32[128,512]{1,0:T(8,128)})) %all-reduce.9.cloned.1.call-update) | async-done | bytes 393232 | tf_op jit(solution)/shard_map/psum | solution.py:25
  227.2 0.0 all-reduce.5.cloned.1.call-update
  227.3 0.0 all-reduce.7.cloned.1.call-start
  227.3 0.0 copy-done.3
  227.3 2.0 fusion.16
  229.3 2.8 reshape.46
  232.1 49.9 %all-reduce.5.cloned.1.call-done = f32[128,512]{1,0:T(8,128)} async-done(((f32[128,512]{1,0:T(8,128)}), f32[128,512]{1,0:T(8,128)}) %all-reduce.5.cloned.1.call-update) | async-done | bytes 262160 | tf_op jit(solution)/shard_map/psum | solution.py:32
  282.0 1.9 fusion.18
  283.9 0.0 all-reduce.7.cloned.1.call-update
  283.9 0.0 reduce-scatter.2.cloned.1.call-start
  283.9 10.1 %fusion.17 = f32[16384,128]{1,0:T(8,128)} fusion(f32[32,16384]{1,0:T(8,128)} %reshape.46, bf16[32,128]{1,0:T(8,128)(2,1)S(1)} %copy-done.4), kind=kOutput, calls=%fused_computation.32 | convolution fusion | flops 805306368 | bytes 10493952 | tf_op jit(solution)/shard_map/dot_general | solution.py:39
  294.0 9.2 %copy.11 = f32[128,64,256]{2,1,0:T(8,128)} copy(f32[128,64,256]{0,2,1:T(8,128)} %bitcast.58) | data formatting | bytes 16777216 | tf_op jit(solution)/shard_map/reshape | solution.py:39
  303.2 0.0 reduce-scatter.2.cloned.1.call-update
  303.2 0.9 copy-done.1
  304.1 0.4 fusion.14
  304.5 0.1 copy.10
  304.6 11.7 %cholesky.44 = f32[128,128]{1,0:T(8,128)S(1)} custom-call(f32[128,128]{1,0:T(8,128)S(1)} %fusion.13), custom_call_target="Cholesky" | custom-call | tf_op jit(solution)/shard_map/jit(cholesky)/cholesky | solution.py:9
  316.4 0.6 compare_reduce_fusion.1
  317.0 0.7 fusion.3
  317.7 9.8 %custom-call.16 = f32[1,128,128]{1,2,0:T(8,128)S(1)} custom-call(f32[1,128,128]{2,1,0:T(8,128)S(1)} %fusion.3), custom_call_target="InvertDiagBlocksLowerTriangular" | custom-call | tf_op jit(solution)/shard_map/jit(_cho_solve)/triangular_solve | solution.py:10
  327.5 0.4 fusion.15
  327.9 0.3 fusion.11
  328.2 0.9 fusion.9
  329.0 1.3 fusion.19
  330.3 0.1 copy.12
  330.4 11.7 %cholesky.55 = f32[128,128]{1,0:T(8,128)S(1)} custom-call(f32[128,128]{1,0:T(8,128)S(1)} %fusion.8), custom_call_target="Cholesky" | custom-call | tf_op jit(solution)/shard_map/jit(cholesky)/cholesky | solution.py:9
  342.2 0.6 compare_reduce_fusion
  342.8 0.7 fusion.4
  343.5 9.8 %custom-call.17 = f32[1,128,128]{1,2,0:T(8,128)S(1)} custom-call(f32[1,128,128]{2,1,0:T(8,128)S(1)} %fusion.4), custom_call_target="InvertDiagBlocksLowerTriangular" | custom-call | tf_op jit(solution)/shard_map/jit(_cho_solve)/triangular_solve | solution.py:10
  353.3 1.2 fusion.6
  354.5 0.3 convolution_bitcast_fusion.1
  354.8 98.3 %reduce-scatter.2.cloned.1.call-done = f32[2,64,256]{2,1,0:T(8,128)} async-done(((f32[128,64,256]{2,1,0:T(8,128)}), f32[2,64,256]{2,1,0:T(8,128)}) %reduce-scatter.2.cloned.1.call-update) | async-done | bytes 131088 | tf_op jit(solution)/shard_map/reduce_scatter | solution.py:38
  453.1 1.8 fusion.20
  454.9 0.7 copy.17
  (13 shorter events, 0.1 us)
Async XLA Ops:
  8.0 1.6 copy-start
  8.0 219.2 %all-reduce.9.cloned.1.call-start = ((), (), s32[]{:S(2)}) async-start(), calls=%async_computation.4 | async-start | bytes 786432 | tf_op jit(solution)/shard_map/psum | solution.py:25
  9.6 55.6 %copy-start.5 = (bf16[64,128]{1,0:T(8,128)(2,1)S(1)}, bf16[64,128]{1,0:T(8,128)(2,1)}, u32[]{:S(2)}) copy-start(bf16[64,128]{1,0:T(8,128)(2,1)} %param.11) | copy-start | bytes 49156
  9.6 55.6 %copy-start.6 = (bf16[32,128]{1,0:T(8,128)(2,1)S(1)}, bf16[32,128]{1,0:T(8,128)(2,1)}, u32[]{:S(2)}) copy-start(bf16[32,128]{1,0:T(8,128)(2,1)} %param.10) | copy-start | bytes 24580
  9.6 55.6 %copy-start.4 = (bf16[32,128]{1,0:T(8,128)(2,1)S(1)}, bf16[32,128]{1,0:T(8,128)(2,1)}, u32[]{:S(2)}) copy-start(bf16[32,128]{1,0:T(8,128)(2,1)} %param.9) | copy-start | bytes 24580
  11.3 216.0 %copy-start.3 = (bf16[512,256]{1,0:T(8,128)(2,1)S(1)}, bf16[512,256]{1,0:T(8,128)(2,1)}, u32[]{:S(2)}) copy-start(bf16[512,256]{1,0:T(8,128)(2,1)} %param.14) | copy-start | bytes 786436
  67.3 214.7 %all-reduce.5.cloned.1.call-start = ((), (), s32[]{:S(2)}) async-start(), calls=%async_computation.2 | async-start | bytes 524288 | tf_op jit(solution)/shard_map/psum | solution.py:32
  227.3 101.8 %all-reduce.7.cloned.1.call-start = ((), (), s32[]{:S(2)}) async-start(), calls=%async_computation.3 | async-start | bytes 262144 | tf_op jit(solution)/shard_map/psum | solution.py:33
  283.9 169.2 %reduce-scatter.2.cloned.1.call-start = ((), (), s32[]{:S(2)}) async-start(), calls=%async_computation.1 | async-start | bytes 8519680 | tf_op jit(solution)/shard_map/reduce_scatter | solution.py:38
  303.2 0.9 copy-start.1
  303.2 151.6 %copy-start.2 = (f32[128,512]{1,0:T(8,128)S(1)}, f32[128,512]{1,0:T(8,128)}, u32[]{:S(2)}) copy-start(f32[128,512]{1,0:T(8,128)} %all-reduce.5.cloned.1.call-done) | copy-start | bytes 786436
Sparse Core Ops, SparseCore 0:
  67.4 159.7 all-reduce.8
  229.6 52.3 all-reduce.4
  285.4 43.6 all-reduce.6
Sparse Core Ops, SparseCore 1:
  303.3 149.7 reduce-scatter.1
